TPU v7x, 512 devices: a whole 4x4x16 slice. The times are simulated.
512 devices in a mesh: band: 16 (over x, y), lon: 32 (over z, core).
Axes of the slice: x: 4, y: 4, z: 16, core: 2. Of those that a mesh axis runs over, the one named last changes fastest.
Arguments:
- back_height: float32 [1024, 8640], P('band', 'lon'), may hold values from -6 to 6
- back_east: float32 [1024, 8640], P('band', 'lon'), may hold values from -6 to 6
- back_north: float32 [1024, 8640], P('band', 'lon'), may hold values from -6 to 6
- obs_values: float32 [65536, 256], P(('band', 'lon')), may hold values from -6 to 6
- obs_owner: int32 [65536, 1], P(('band', 'lon')), may hold values from 0 to 31; in each aligned block of 128 rows (0 to 127, 128 to 255, ...) at most 12 rows name the same one
- obs_row: int32 [65536], P(('band', 'lon')), may hold values from 0 to 63
- obs_count: int32 [65536], P(('band', 'lon')), may hold values from 1 to 256
- polar_mask: int32 [1024], P('band'), may hold values from 0 to 1, as said below
- keep_share: float32 [1024], P('band'), may hold values from 0.05 to 0.9
- depth_level: int32 [1024, 8640], P('band', 'lon'), may hold values from 0 to 50
Outputs:
- grad_height: float32 [1024, 8640], P('band', 'lon')
- grad_east: float32 [1024, 8640], P('band', 'lon')
- grad_north: float32 [1024, 8640], P('band', 'lon')
Inputs may be any that keep to these rules, and one draw needn't show every extreme that they name: `obs_owner`: among the rows of one device at most 12 name the same tile, a bound that some block reaches. `polar_mask`: among the 64 rows of one band at most 32 are 1, and some band has exactly 32.
All inputs are finite; a program needn't handle non-finite values.
Results may differ from a plain program's by a relative error of at most 0.00005.
Values sent between devices are 32-bit elements; how exact they have to be, the bound alone decides.
No kernel may reach another device: no remote copies, remote signals or barrier semaphores. Data moves between devices by JAX's collectives and lax.ppermute only.
A program may use at most 64 MiB of HBM per device.

v0:
```python
import math
import jax
import jax.numpy as jnp
from jax import lax
from jax.sharding import PartitionSpec as P

MODES = 128
LEVELS = 50
COURANT = 0.25
ROTATION = 0.4
LIMIT = 1.3089969389957472
OUTER_COUNT = 64


def with_halo(cells, sides, width, closed):
    for axis, dim in sides:
        count = lax.axis_size(axis)
        ends = count if closed else count - 1
        head = lax.slice_in_dim(cells, 0, width, axis=dim)
        tail = lax.slice_in_dim(cells, cells.shape[dim] - width, cells.shape[dim], axis=dim)
        cells = jnp.concatenate(
            [
                lax.ppermute(tail, axis, [(i, (i + 1) % count) for i in range(ends)]),
                cells,
                lax.ppermute(head, axis, [((i + 1) % count, i) for i in range(ends)]),
            ],
            axis=dim,
        )
    return cells


def latitude_terms(first_row, count_rows, total_rows):
    global_rows = first_row + jnp.arange(count_rows, dtype=jnp.int32)
    centre = (global_rows.astype(jnp.float32) + 0.5) / total_rows
    angle = (2.0 * centre - 1.0) * LIMIT
    return (1.0 / jnp.cos(angle), ROTATION * jnp.sin(angle))


def spectral_tables(length, modes):
    inner_count = length // OUTER_COUNT
    outer_pos = jnp.arange(OUTER_COUNT, dtype=jnp.int32)
    outer_phase = outer_pos[:, None] * outer_pos[None, :] % OUTER_COUNT
    outer_angle = outer_phase.astype(jnp.float32) * (2.0 * math.pi / OUTER_COUNT)
    number = jnp.arange(modes, dtype=jnp.int32)
    inner_pos = jnp.arange(inner_count, dtype=jnp.int32)
    inner_phase = number[:, None] * inner_pos[None, :] % length
    inner_angle = inner_phase.astype(jnp.float32) * (2.0 * math.pi / length)
    grouping = (number[:, None] % OUTER_COUNT == outer_pos[None, :]).astype(jnp.float32)
    mode_weights = jnp.where(number == 0, 1.0 / length, 2.0 / length).astype(jnp.float32)
    return (
        jnp.cos(outer_angle),
        jnp.sin(outer_angle),
        jnp.cos(inner_angle),
        jnp.sin(inner_angle),
        grouping,
        mode_weights,
    )


def project_rows(pieces, tables):
    cos_outer, sin_outer, cos_inner, sin_inner, grouping, mode_weights = tables
    fields, rows, length = pieces.shape
    inner_count = length // OUTER_COUNT
    highest = lax.Precision.HIGHEST
    split = pieces.reshape(fields, rows, OUTER_COUNT, inner_count)
    real_part = jnp.einsum("fnab,ar->fnrb", split, cos_outer, precision=highest)
    imag_part = -jnp.einsum("fnab,ar->fnrb", split, sin_outer, precision=highest)
    real_mode = jnp.einsum("fnrb,mr->fnmb", real_part, grouping, precision=highest)
    imag_mode = jnp.einsum("fnrb,mr->fnmb", imag_part, grouping, precision=highest)
    coeff_real = jnp.sum(real_mode * cos_inner + imag_mode * sin_inner, axis=3) * mode_weights
    coeff_imag = jnp.sum(imag_mode * cos_inner - real_mode * sin_inner, axis=3) * mode_weights
    back_real = coeff_real[..., None] * cos_inner - coeff_imag[..., None] * sin_inner
    back_imag = coeff_real[..., None] * sin_inner + coeff_imag[..., None] * cos_inner
    group_real = jnp.einsum("fnmb,mr->fnrb", back_real, grouping, precision=highest)
    group_imag = jnp.einsum("fnmb,mr->fnrb", back_imag, grouping, precision=highest)
    result = jnp.einsum("fnrb,ar->fnab", group_real, cos_outer, precision=highest) - jnp.einsum(
        "fnrb,ar->fnab", group_imag, sin_outer, precision=highest
    )
    return result.reshape(fields, rows, length)


def extend(stacked, width):
    wider = with_halo(stacked, (("lon", 2),), width, True)
    return with_halo(wider, (("band", 1),), width, False)


def polar_filter(stacked, weight, tables):
    smooth = project_rows(
        lax.all_to_all(stacked, "lon", split_axis=1, concat_axis=2, tiled=True), tables
    )
    projected = lax.all_to_all(smooth, "lon", split_axis=2, concat_axis=1, tiled=True)
    return stacked + weight[None, :, None] * (projected - stacked)


def adjoint_step(state, weight, tables, wet_cells, depth_share, metric, rotation):
    stacked = jnp.stack([state[0], wet_cells * state[1], wet_cells * state[2]])
    kept = polar_filter(stacked, weight, tables)
    height_kept = kept[0]
    east_kept = kept[1]
    north_kept = kept[2]
    wider = extend(kept[1:], 1)
    middle = height_kept + COURANT * (
        metric[:, None] * (wider[0, 1:-1, 2:] - wider[0, 1:-1, :-2]) * 0.5
        + (wider[1, 2:, 1:-1] - wider[1, :-2, 1:-1]) * 0.5
    )
    beside_all = extend(middle[None], 1)[0]
    new_east = (
        east_kept
        - rotation[:, None] * north_kept
        + COURANT
        * depth_share
        * (metric[:, None] * (beside_all[1:-1, 2:] - beside_all[1:-1, :-2]) * 0.5)
    )
    new_north = (
        north_kept
        + rotation[:, None] * east_kept
        + COURANT * depth_share * ((beside_all[2:, 1:-1] - beside_all[:-2, 1:-1]) * 0.5)
    )
    return (middle, new_east, new_north)


def place_observations(
    obs_values, obs_owner, obs_row, obs_count, lon_count, count_rows, count_cols
):
    sample_rows, sample_width = obs_values.shape
    capacity = 3 * sample_rows // lon_count
    owner_ids = obs_owner[:, 0]
    owner_hits = (owner_ids[:, None] == jnp.arange(lon_count, dtype=jnp.int32)[None, :]).astype(
        jnp.int32
    )
    arrival = jnp.sum((jnp.cumsum(owner_hits, axis=0) - 1) * owner_hits, axis=1)
    target = owner_ids * capacity + arrival
    outgoing = (
        jnp.zeros((lon_count * capacity, sample_width), jnp.float32).at[target].set(obs_values)
    )
    labels = (
        jnp.zeros((lon_count * capacity, 2), jnp.int32)
        .at[target]
        .set(jnp.stack([obs_row, obs_count], axis=1))
    )
    incoming, tagged = (
        lax.all_to_all(
            outgoing.reshape(lon_count, capacity, sample_width),
            "lon",
            split_axis=0,
            concat_axis=0,
            tiled=True,
        ),
        lax.all_to_all(
            labels.reshape(lon_count, capacity, 2), "lon", split_axis=0, concat_axis=0, tiled=True
        ),
    )
    flat_values = incoming.reshape(lon_count * capacity, sample_width)
    flat_labels = tagged.reshape(lon_count * capacity, 2)
    alive_cells = jnp.arange(sample_width, dtype=jnp.int32)[None, :] < flat_labels[:, 1:2]
    summed = jax.ops.segment_sum(
        jnp.where(alive_cells, flat_values, 0.0), flat_labels[:, 0], num_segments=count_rows
    )
    return jnp.pad(summed, ((0, 0), (0, count_cols - sample_width)))


def on_device(
    back_height,
    back_east,
    back_north,
    obs_values,
    obs_owner,
    obs_row,
    obs_count,
    polar_mask,
    keep_share,
    depth_level,
):
    count_rows, count_cols = back_height.shape
    band_count = lax.axis_size("band")
    lon_count = lax.axis_size("lon")
    total_rows = count_rows * band_count
    first_row = lax.axis_index("band") * count_rows
    metric, rotation = latitude_terms(first_row, count_rows, total_rows)
    wet_cells = (depth_level > 0).astype(jnp.float32)
    depth_share = depth_level.astype(jnp.float32) / LEVELS
    weight = polar_mask.astype(jnp.float32) * (1.0 - keep_share)
    tables = spectral_tables(count_cols * lon_count, MODES)
    placed = place_observations(
        obs_values, obs_owner, obs_row, obs_count, lon_count, count_rows, count_cols
    )
    state = (back_height, back_east, back_north)
    state = adjoint_step(state, weight, tables, wet_cells, depth_share, metric, rotation)
    state = (state[0] + placed, state[1], state[2])
    state = adjoint_step(state, weight, tables, wet_cells, depth_share, metric, rotation)
    return (state[0], state[1], state[2])


def solution(mesh):
    placed = (
        P("band", "lon"),
        P("band", "lon"),
        P("band", "lon"),
        P(("band", "lon"), None),
        P(("band", "lon"), None),
        P(("band", "lon")),
        P(("band", "lon")),
        P("band"),
        P("band"),
        P("band", "lon"),
    )
    return jax.shard_map(
        on_device,
        mesh=mesh,
        in_specs=placed,
        out_specs=(P("band", "lon"), P("band", "lon"), P("band", "lon")),
        check_vma=False,
    )
```

profile of v0, /device:TPU:26, one launch (start us, length us, event | category | flops | bytes accessed | tf_op | source)
XLA Modules:
  0.0 317.1 jit_solution(5938740981193499104)
XLA Ops:
  3.5 15.5 %all-to-all-start = ((f32[3,64,270]{2,0,1:T(4,128)}), f32[3,64,270]{2,0,1:T(4,128)S(1)}, u32[]{:S(2)}, u32[]{:S(2)}) async-start(f32[3,64,270]{2,0,1:T(4,128)} %copy.81), calls=%async_computation | async-start | bytes 786432 | tf_op jit(solution)/shard_map/all_to_all | solution.py:89
  24.3 22.9 %all-to-all-done = f32[3,64,270]{2,0,1:T(4,128)S(1)} async-done(((f32[3,64,270]{2,0,1:T(4,128)}), f32[3,64,270]{2,0,1:T(4,128)S(1)}, u32[]{:S(2)}, u32[]{:S(2)}) %all-to-all-start) | async-done | bytes 207392 | tf_op jit(solution)/shard_map/all_to_all | solution.py:89
  47.2 3.9 %all-to-all-start.2 = ((s32[32,12,2]{1,2,0:T(2,128)}), s32[32,12,2]{1,2,0:T(2,128)S(1)}, u32[]{:S(2)}, u32[]{:S(2)}) async-start(s32[32,12,2]{1,2,0:T(2,128)} %copy.89), calls=%async_computation.2 | async-start | bytes 65536 | tf_op jit(solution)/shard_map/all_to_all | solution.py:149
  56.3 11.0 %copy.106 = f32[3,2,64,135]{0,1,3,2:T(2,128)} copy(f32[3,2,64,135]{3,2,1,0:T(8,128)S(1)} %fusion.2) | data formatting | bytes 414720 | tf_op jit(solution)/shard_map/reshape | solution.py:79
  67.3 11.7 %reshape.177 = f32[32,1,1620]{2,1,0:T(1,128)} reshape(f32[8640,2,3]{2,1,0:T(2,128)} %bitcast.184) | data formatting | bytes 414720
  79.0 12.2 %all-to-all-start.1 = ((f32[32,1,1620]{2,1,0:T(1,128)}), f32[32,1,1620]{2,1,0:T(1,128)S(1)}, u32[]{:S(2)}, u32[]{:S(2)}) async-start(f32[32,1,1620]{2,1,0:T(1,128)} %reshape.177), calls=%async_computation.1 | async-start | bytes 425984 | tf_op jit(solution)/shard_map/all_to_all | solution.py:91
  93.6 18.3 %all-to-all-done.1 = f32[32,1,1620]{2,1,0:T(1,128)S(1)} async-done(((f32[32,1,1620]{2,1,0:T(1,128)}), f32[32,1,1620]{2,1,0:T(1,128)S(1)}, u32[]{:S(2)}, u32[]{:S(2)}) %all-to-all-start.1) | async-done | bytes 207392 | tf_op jit(solution)/shard_map/all_to_all | solution.py:91
  111.9 4.1 %all-to-all-start.3 = ((f32[32,12,256]{2,1,0:T(8,128)}), f32[32,12,256]{2,1,0:T(8,128)S(1)}, u32[]{:S(2)}, u32[]{:S(2)}) async-start(f32[32,12,256]{2,1,0:T(8,128)} %reshape.134), calls=%async_computation.3 | async-start | bytes 1048576 | tf_op jit(solution)/shard_map/all_to_all | solution.py:142
  117.7 8.1 %reshape.178 = f32[8640,2,3]{2,1,0:T(2,128)} reshape(f32[32,1620]{1,0:T(8,128)S(1)} %reduce.8) | data formatting | bytes 414720
  125.8 11.2 %copy.86 = f32[3,2,32,270]{3,1,2,0:T(2,128)S(1)} copy(f32[3,2,32,270]{0,1,3,2:T(2,128)} %bitcast.185) | data formatting | bytes 414720 | tf_op jit(solution)/shard_map/all_to_all | solution.py:91
  141.9 3.1 collective-permute-done.1
  147.8 5.3 %collective-permute-start.3 = (f32[2,1,272]{2,1,0:T(1,128)S(1)}, f32[2,1,272]{2,1,0:T(1,128)S(1)}, u32[]{:S(2)}, u32[]{:S(2)}) collective-permute-start(f32[2,1,272]{2,1,0:T(1,128)S(1)} %get-tuple-element.22), channel_id=1, source_target_pairs={{0,32},{32,64},{64,96},{96,128},{128,160},{160,192},{192,224},{224... | collective-permute-start | bytes 6536 | tf_op jit(solution)/shard_map/ppermute | solution.py:23
  161.1 4.6 %collective-permute-start.6 = (f32[1,1,272]{2,1,0:T(1,128)S(1)}, f32[1,1,272]{2,1,0:T(1,128)S(1)}, u32[]{:S(2)}, u32[]{:S(2)}) collective-permute-start(f32[1,1,272]{2,1,0:T(1,128)S(1)} %get-tuple-element.30), channel_id=1, source_target_pairs={{0,32},{32,64},{64,96},{96,128},{128,160},{160,192},{192,224},{224... | collective-permute-start | bytes 3272 | tf_op jit(solution)/shard_map/ppermute | solution.py:23
  167.7 5.6 %collective-permute-done.7 = f32[1,1,272]{2,1,0:T(1,128)S(1)} collective-permute-done((f32[1,1,272]{2,1,0:T(1,128)S(1)}, f32[1,1,272]{2,1,0:T(1,128)S(1)}, u32[]{:S(2)}, u32[]{:S(2)}) %collective-permute-start.7) | collective-permute-done | bytes 1120 | tf_op jit(solution)/shard_map/ppermute | solution.py:25
  173.8 37.5 %all_to_all.76 = f32[3,64,270]{2,0,1:T(4,128)S(1)} all-to-all(f32[3,64,270]{2,0,1:T(4,128)S(1)} %copy.91), channel_id=1, replica_groups=mesh['band'=16,'lon'=32] {'lon'}, dimensions={1} | all-to-all | bytes 414720 | tf_op jit(solution)/shard_map/all_to_all | solution.py:89
  216.5 11.0 %copy.109 = f32[3,2,64,135]{0,1,3,2:T(2,128)} copy(f32[3,2,64,135]{3,2,1,0:T(8,128)S(1)} %fusion) | data formatting | bytes 414720 | tf_op jit(solution)/shard_map/reshape | solution.py:79
  227.5 11.1 %reshape.179 = f32[32,1,1620]{2,1,0:T(1,128)S(1)} reshape(f32[8640,2,3]{2,1,0:T(2,128)} %bitcast.186) | data formatting | bytes 414720
  238.6 23.7 %all_to_all.77 = f32[32,1,1620]{2,1,0:T(1,128)S(1)} all-to-all(f32[32,1,1620]{2,1,0:T(1,128)S(1)} %reshape.179), channel_id=1, replica_groups=mesh['band'=16,'lon'=32] {'lon'}, dimensions={0} | all-to-all | bytes 414720 | tf_op jit(solution)/shard_map/all_to_all | solution.py:91
  263.4 8.1 %reshape.180 = f32[8640,2,3]{2,1,0:T(2,128)} reshape(f32[32,1620]{1,0:T(8,128)S(1)} %reduce.9) | data formatting | bytes 414720
  271.5 11.1 %copy.96 = f32[3,2,32,270]{3,1,2,0:T(2,128)S(1)} copy(f32[3,2,32,270]{0,1,3,2:T(2,128)} %bitcast.187) | data formatting | bytes 414720 | tf_op jit(solution)/shard_map/all_to_all | solution.py:91
  285.0 3.0 collective-permute-done.9
  290.0 6.0 %collective-permute-start.11 = (f32[2,1,272]{2,1,0:T(1,128)S(1)}, f32[2,1,272]{2,1,0:T(1,128)S(1)}, u32[]{:S(2)}, u32[]{:S(2)}) collective-permute-start(f32[2,1,272]{2,1,0:T(1,128)S(1)} %get-tuple-element.20), channel_id=1, source_target_pairs={{0,32},{32,64},{64,96},{96,128},{128,160},{160,192},{192,224},{224... | collective-permute-start | bytes 6536 | tf_op jit(solution)/shard_map/ppermute | solution.py:23
  302.3 6.3 %collective-permute-start.14 = (f32[1,1,272]{2,1,0:T(1,128)S(1)}, f32[1,1,272]{2,1,0:T(1,128)S(1)}, u32[]{:S(2)}, u32[]{:S(2)}) collective-permute-start(f32[1,1,272]{2,1,0:T(1,128)S(1)} %get-tuple-element.28), channel_id=1, source_target_pairs={{0,32},{32,64},{64,96},{96,128},{128,160},{160,192},{192,224},{224... | collective-permute-start | bytes 3272 | tf_op jit(solution)/shard_map/ppermute | solution.py:23
  310.5 5.6 %collective-permute-done.15 = f32[1,1,272]{2,1,0:T(1,128)S(1)} collective-permute-done((f32[1,1,272]{2,1,0:T(1,128)S(1)}, f32[1,1,272]{2,1,0:T(1,128)S(1)}, u32[]{:S(2)}, u32[]{:S(2)}) %collective-permute-start.15) | collective-permute-done | bytes 1120 | tf_op jit(solution)/shard_map/ppermute | solution.py:25
  (108 shorter events, 55.1 us)
Async XLA Ops:
  3.5 43.7 %all-to-all-start = ((f32[3,64,270]{2,0,1:T(4,128)}), f32[3,64,270]{2,0,1:T(4,128)S(1)}, u32[]{:S(2)}, u32[]{:S(2)}) async-start(f32[3,64,270]{2,0,1:T(4,128)} %copy.81), calls=%async_computation | async-start | bytes 786432 | tf_op jit(solution)/shard_map/all_to_all | solution.py:89
  47.2 31.8 %all-to-all-start.2 = ((s32[32,12,2]{1,2,0:T(2,128)}), s32[32,12,2]{1,2,0:T(2,128)S(1)}, u32[]{:S(2)}, u32[]{:S(2)}) async-start(s32[32,12,2]{1,2,0:T(2,128)} %copy.89), calls=%async_computation.2 | async-start | bytes 65536 | tf_op jit(solution)/shard_map/all_to_all | solution.py:149
  56.3 59.7 %copy-start.2 = (f32[64]{0:T(128)S(1)}, f32[64]{0:T(128)}, u32[]{:S(2)}) copy-start(f32[64]{0:T(128)} %param.18) | copy-start | bytes 772
  56.3 59.7 %copy-start.3 = (s32[64]{0:T(128)S(1)}, s32[64]{0:T(128)}, u32[]{:S(2)}) copy-start(s32[64]{0:T(128)} %param.17) | copy-start | bytes 772
  79.0 32.9 %all-to-all-start.1 = ((f32[32,1,1620]{2,1,0:T(1,128)}), f32[32,1,1620]{2,1,0:T(1,128)S(1)}, u32[]{:S(2)}, u32[]{:S(2)}) async-start(f32[32,1,1620]{2,1,0:T(1,128)} %reshape.177), calls=%async_computation.1 | async-start | bytes 425984 | tf_op jit(solution)/shard_map/all_to_all | solution.py:91
  111.9 41.3 %all-to-all-start.3 = ((f32[32,12,256]{2,1,0:T(8,128)}), f32[32,12,256]{2,1,0:T(8,128)S(1)}, u32[]{:S(2)}, u32[]{:S(2)}) async-start(f32[32,12,256]{2,1,0:T(8,128)} %reshape.134), calls=%async_computation.3 | async-start | bytes 1048576 | tf_op jit(solution)/shard_map/all_to_all | solution.py:142
  117.6 19.5 %copy-start.1 = (f32[64,270]{1,0:T(8,128)S(1)}, f32[64,270]{1,0:T(8,128)}, u32[]{:S(2)}) copy-start(f32[64,270]{1,0:T(8,128)} %param.10) | copy-start | bytes 207364
  125.8 47.6 %copy-start = (s32[64,270]{1,0:T(8,128)S(1)}, s32[64,270]{1,0:T(8,128)}, u32[]{:S(2)}) copy-start(s32[64,270]{1,0:T(8,128)} %param.19) | copy-start | bytes 207364
  137.3 4.6 %collective-permute-start = (f32[2,64,1]{2,1,0:T(8,128)S(1)}, f32[2,64,1]{2,1,0:T(8,128)S(1)}, u32[]{:S(2)}, u32[]{:S(2)}) collective-permute-start(f32[2,64,1]{2,1,0:T(8,128)S(1)} %get-tuple-element.26), channel_id=1, source_target_pairs={{1,0},{2,1},{3,2},{4,3},{5,4},{6,5},{7,6},{8,7},{9,8},{10,9},{11,1... | collective-permute-start | bytes 1544 | tf_op jit(solution)/shard_map/ppermute | solution.py:25
  140.0 5.0 %collective-permute-start.1 = (f32[2,64,1]{2,1,0:T(8,128)S(1)}, f32[2,64,1]{2,1,0:T(8,128)S(1)}, u32[]{:S(2)}, u32[]{:S(2)}) collective-permute-start(f32[2,64,1]{2,1,0:T(8,128)S(1)} %get-tuple-element.27), channel_id=1, source_target_pairs={{0,1},{1,2},{2,3},{3,4},{4,5},{5,6},{6,7},{7,8},{8,9},{9,10},{10,1... | collective-permute-start | bytes 1544 | tf_op jit(solution)/shard_map/ppermute | solution.py:23
  145.1 10.9 %collective-permute-start.2 = (f32[2,1,272]{2,1,0:T(1,128)S(1)}, f32[2,1,272]{2,1,0:T(1,128)S(1)}, u32[]{:S(2)}, u32[]{:S(2)}) collective-permute-start(f32[2,1,272]{2,1,0:T(1,128)S(1)} %get-tuple-element.21), channel_id=1, source_target_pairs={{32,0},{64,32},{96,64},{128,96},{160,128},{192,160},{224,192},{256... | collective-permute-start | bytes 6536 | tf_op jit(solution)/shard_map/ppermute | solution.py:25
  147.8 8.3 %collective-permute-start.3 = (f32[2,1,272]{2,1,0:T(1,128)S(1)}, f32[2,1,272]{2,1,0:T(1,128)S(1)}, u32[]{:S(2)}, u32[]{:S(2)}) collective-permute-start(f32[2,1,272]{2,1,0:T(1,128)S(1)} %get-tuple-element.22), channel_id=1, source_target_pairs={{0,32},{32,64},{64,96},{96,128},{128,160},{160,192},{192,224},{224... | collective-permute-start | bytes 6536 | tf_op jit(solution)/shard_map/ppermute | solution.py:23
  156.4 4.6 %collective-permute-start.4 = (f32[1,64,1]{2,1,0:T(8,128)S(1)}, f32[1,64,1]{2,1,0:T(8,128)S(1)}, u32[]{:S(2)}, u32[]{:S(2)}) collective-permute-start(f32[1,64,1]{2,1,0:T(8,128)S(1)} %get-tuple-element.34), channel_id=1, source_target_pairs={{0,1},{1,2},{2,3},{3,4},{4,5},{5,6},{6,7},{7,8},{8,9},{9,10},{10,1... | collective-permute-start | bytes 776 | tf_op jit(solution)/shard_map/ppermute | solution.py:23
  156.5 4.6 %collective-permute-start.5 = (f32[1,64,1]{2,1,0:T(8,128)S(1)}, f32[1,64,1]{2,1,0:T(8,128)S(1)}, u32[]{:S(2)}, u32[]{:S(2)}) collective-permute-start(f32[1,64,1]{2,1,0:T(8,128)S(1)} %get-tuple-element.35), channel_id=1, source_target_pairs={{1,0},{2,1},{3,2},{4,3},{5,4},{6,5},{7,6},{8,7},{9,8},{10,9},{11,1... | collective-permute-start | bytes 776 | tf_op jit(solution)/shard_map/ppermute | solution.py:25
  161.1 6.6 %collective-permute-start.6 = (f32[1,1,272]{2,1,0:T(1,128)S(1)}, f32[1,1,272]{2,1,0:T(1,128)S(1)}, u32[]{:S(2)}, u32[]{:S(2)}) collective-permute-start(f32[1,1,272]{2,1,0:T(1,128)S(1)} %get-tuple-element.30), channel_id=1, source_target_pairs={{0,32},{32,64},{64,96},{96,128},{128,160},{160,192},{192,224},{224... | collective-permute-start | bytes 3272 | tf_op jit(solution)/shard_map/ppermute | solution.py:23
  165.7 7.6 %collective-permute-start.7 = (f32[1,1,272]{2,1,0:T(1,128)S(1)}, f32[1,1,272]{2,1,0:T(1,128)S(1)}, u32[]{:S(2)}, u32[]{:S(2)}) collective-permute-start(f32[1,1,272]{2,1,0:T(1,128)S(1)} %get-tuple-element.31), channel_id=1, source_target_pairs={{32,0},{64,32},{96,64},{128,96},{160,128},{192,160},{224,192},{256... | collective-permute-start | bytes 3272 | tf_op jit(solution)/shard_map/ppermute | solution.py:25
  283.1 1.9 collective-permute-start.8
  283.1 4.9 %collective-permute-start.9 = (f32[2,64,1]{2,1,0:T(8,128)S(1)}, f32[2,64,1]{2,1,0:T(8,128)S(1)}, u32[]{:S(2)}, u32[]{:S(2)}) collective-permute-start(f32[2,64,1]{2,1,0:T(8,128)S(1)} %get-tuple-element.25), channel_id=1, source_target_pairs={{0,1},{1,2},{2,3},{3,4},{4,5},{5,6},{6,7},{7,8},{8,9},{9,10},{10,1... | collective-permute-start | bytes 1544 | tf_op jit(solution)/shard_map/ppermute | solution.py:23
  288.1 8.0 %collective-permute-start.10 = (f32[2,1,272]{2,1,0:T(1,128)S(1)}, f32[2,1,272]{2,1,0:T(1,128)S(1)}, u32[]{:S(2)}, u32[]{:S(2)}) collective-permute-start(f32[2,1,272]{2,1,0:T(1,128)S(1)} %get-tuple-element.19), channel_id=1, source_target_pairs={{32,0},{64,32},{96,64},{128,96},{160,128},{192,160},{224,192},{256... | collective-permute-start | bytes 6536 | tf_op jit(solution)/shard_map/ppermute | solution.py:25
  290.0 7.3 %collective-permute-start.11 = (f32[2,1,272]{2,1,0:T(1,128)S(1)}, f32[2,1,272]{2,1,0:T(1,128)S(1)}, u32[]{:S(2)}, u32[]{:S(2)}) collective-permute-start(f32[2,1,272]{2,1,0:T(1,128)S(1)} %get-tuple-element.20), channel_id=1, source_target_pairs={{0,32},{32,64},{64,96},{96,128},{128,160},{160,192},{192,224},{224... | collective-permute-start | bytes 6536 | tf_op jit(solution)/shard_map/ppermute | solution.py:23
  297.6 4.6 %collective-permute-start.12 = (f32[1,64,1]{2,1,0:T(8,128)S(1)}, f32[1,64,1]{2,1,0:T(8,128)S(1)}, u32[]{:S(2)}, u32[]{:S(2)}) collective-permute-start(f32[1,64,1]{2,1,0:T(8,128)S(1)} %get-tuple-element.32), channel_id=1, source_target_pairs={{0,1},{1,2},{2,3},{3,4},{4,5},{5,6},{6,7},{7,8},{8,9},{9,10},{10,1... | collective-permute-start | bytes 776 | tf_op jit(solution)/shard_map/ppermute | solution.py:23
  297.6 4.6 %collective-permute-start.13 = (f32[1,64,1]{2,1,0:T(8,128)S(1)}, f32[1,64,1]{2,1,0:T(8,128)S(1)}, u32[]{:S(2)}, u32[]{:S(2)}) collective-permute-start(f32[1,64,1]{2,1,0:T(8,128)S(1)} %get-tuple-element.33), channel_id=1, source_target_pairs={{1,0},{2,1},{3,2},{4,3},{5,4},{6,5},{7,6},{8,7},{9,8},{10,9},{11,1... | collective-permute-start | bytes 776 | tf_op jit(solution)/shard_map/ppermute | solution.py:25
  302.3 8.2 %collective-permute-start.14 = (f32[1,1,272]{2,1,0:T(1,128)S(1)}, f32[1,1,272]{2,1,0:T(1,128)S(1)}, u32[]{:S(2)}, u32[]{:S(2)}) collective-permute-start(f32[1,1,272]{2,1,0:T(1,128)S(1)} %get-tuple-element.28), channel_id=1, source_target_pairs={{0,32},{32,64},{64,96},{96,128},{128,160},{160,192},{192,224},{224... | collective-permute-start | bytes 3272 | tf_op jit(solution)/shard_map/ppermute | solution.py:23
  308.6 7.6 %collective-permute-start.15 = (f32[1,1,272]{2,1,0:T(1,128)S(1)}, f32[1,1,272]{2,1,0:T(1,128)S(1)}, u32[]{:S(2)}, u32[]{:S(2)}) collective-permute-start(f32[1,1,272]{2,1,0:T(1,128)S(1)} %get-tuple-element.29), channel_id=1, source_target_pairs={{32,0},{64,32},{96,64},{128,96},{160,128},{192,160},{224,192},{256... | collective-permute-start | bytes 3272 | tf_op jit(solution)/shard_map/ppermute | solution.py:25
where the time goes:
time: 318 us; the launch traced here: 317 us
  local copies, waits for them, and re-layouts  90.5 us (28%)
  starting transfers between devices  75.3 us (24%)
  waiting for transfers between devices  66.2 us (21%)
  blocking collectives  61.2 us (19%)
  other arithmetic  12.8 us (4%)
  matrix products  9.91 us (3%)
    unnamed x12, local copies, waits for them, and re-layouts  39 us
    all_to_all x1, blocking collectives, polar_filter(): lax.all_to_all(stacked, 'lon', split_axis=1, concat_axis=2, tiled=True)  37.5 us
    all_to_all x1, blocking collectives, polar_filter(): lax.all_to_all(smooth, 'lon', split_axis=2, concat_axis=1, tiled=True)  23.7 us
    all_to_all x5, local copies, waits for them, and re-layouts, polar_filter(): lax.all_to_all(smooth, 'lon', split_axis=2, concat_axis=1, tiled=True)  23.3 us
    all_to_all x1, waiting for transfers between devices, polar_filter(): lax.all_to_all(stacked, 'lon', split_axis=1, concat_axis=2, tiled=True)  22.9 us
    ppermute x8, starting transfers between devices, with_halo(): lax.ppermute(tail, axis, [(i, (i + 1) % count) for i in range(ends)])  22.7 us
    reshape x2, local copies, waits for them, and re-layouts, project_rows(): return result.reshape(fields, rows, length)  22 us
    all_to_all x1, waiting for transfers between devices, polar_filter(): lax.all_to_all(smooth, 'lon', split_axis=2, concat_axis=1, tiled=True)  18.3 us
  transfers between devices with their start and end apart: 20, of which 11 were waited for; matrix products, arithmetic and copies ran while one was open for 19% of the time, Pallas kernels for 0%

commit v1 on v0

--- a/solution.py
+++ b/solution.py
@@ -88,7 +88,10 @@
     smooth = project_rows(
         lax.all_to_all(stacked, "lon", split_axis=1, concat_axis=2, tiled=True), tables
     )
-    projected = lax.all_to_all(smooth, "lon", split_axis=2, concat_axis=1, tiled=True)
+    projected = jnp.concatenate(
+        lax.all_to_all(jnp.stack(jnp.split(smooth, lax.axis_size("lon"), axis=2)), "lon", 0, 0),
+        axis=1,
+    )
     return stacked + weight[None, :, None] * (projected - stacked)
 
 

time: 318 us -> 284 us (0.89)
  the two profiles are of different devices: /device:TPU:26 before, /device:TPU:4 now
where the time goes in v1:
time: 284 us
  waiting for transfers between devices  90.9 us (32%)
  starting transfers between devices  74.1 us (26%)
  blocking collectives  66.6 us (23%)
  local copies, waits for them, and re-layouts  33.7 us (12%)
  matrix products  9.92 us (3%)
  other arithmetic  7.01 us (2%)
    ppermute x8, waiting for transfers between devices, with_halo(): lax.ppermute(tail, axis, [(i, (i + 1) % count) for i in range(ends)])  40.9 us
    all_to_all x1, blocking collectives, polar_filter(): lax.all_to_all(stacked, 'lon', split_axis=1, concat_axis=2, tiled=True)  39.5 us
    ppermute x8, starting transfers between devices, with_halo(): lax.ppermute(head, axis, [((i + 1) % count, i) for i in range(ends)])  28.7 us
    all_to_all x1, blocking collectives, polar_filter(): lax.all_to_all(jnp.stack(jnp.split(smooth, lax.axis_size('lon'), axis=2))...  27.2 us
    unnamed x76, local copies, waits for them, and re-layouts  25.4 us
    all_to_all x1, waiting for transfers between devices, polar_filter(): lax.all_to_all(stacked, 'lon', split_axis=1, concat_axis=2, tiled=True)  24.2 us
    all_to_all x1, waiting for transfers between devices, polar_filter(): lax.all_to_all(jnp.stack(jnp.split(smooth, lax.axis_size('lon'), axis=2))...  21.8 us
    all_to_all x1, starting transfers between devices, polar_filter(): lax.all_to_all(stacked, 'lon', split_axis=1, concat_axis=2, tiled=True)  15.5 us
  transfers between devices with their start and end apart: 20, of which 11 were waited for; matrix products, arithmetic and copies ran while one was open for 13% of the time, Pallas kernels for 0%

profile of v1, /device:TPU:4, one launch (start us, length us, event | category | flops | bytes accessed | tf_op | source)
XLA Modules:
  0.0 283.5 jit_solution(6184320111131222681)
XLA Ops:
  2.7 15.5 %all-to-all-start = ((f32[3,64,270]{2,0,1:T(4,128)}), f32[3,64,270]{2,0,1:T(4,128)S(1)}, u32[]{:S(2)}, u32[]{:S(2)}) async-start(f32[3,64,270]{2,0,1:T(4,128)} %copy.129), calls=%async_computation | async-start | bytes 786432 | tf_op jit(solution)/shard_map/all_to_all | solution.py:89
  22.2 24.2 %all-to-all-done = f32[3,64,270]{2,0,1:T(4,128)S(1)} async-done(((f32[3,64,270]{2,0,1:T(4,128)}), f32[3,64,270]{2,0,1:T(4,128)S(1)}, u32[]{:S(2)}, u32[]{:S(2)}) %all-to-all-start) | async-done | bytes 207392 | tf_op jit(solution)/shard_map/all_to_all | solution.py:89
  46.4 3.9 %all-to-all-start.2 = ((s32[32,12,2]{1,2,0:T(2,128)}), s32[32,12,2]{1,2,0:T(2,128)S(1)}, u32[]{:S(2)}, u32[]{:S(2)}) async-start(s32[32,12,2]{1,2,0:T(2,128)} %copy.136), calls=%async_computation.2 | async-start | bytes 65536 | tf_op jit(solution)/shard_map/all_to_all | solution.py:152
  77.4 12.2 %all-to-all-start.1 = ((f32[32,3,2,270]{3,2,1,0:T(2,128)}), f32[32,3,2,270]{3,2,1,0:T(2,128)S(1)}, u32[]{:S(2)}, u32[]{:S(2)}) async-start(f32[32,3,2,270]{3,2,1,0:T(2,128)} %constant_dynamic-update-slice_fusion), calls=%async_computation.1 | async-start | bytes 589824 | tf_op jit(solution)/shard_map/all_to_all | solution.py:92
  91.9 21.8 %all-to-all-done.1 = f32[32,3,2,270]{3,2,1,0:T(2,128)S(1)} async-done(((f32[32,3,2,270]{3,2,1,0:T(2,128)}), f32[32,3,2,270]{3,2,1,0:T(2,128)S(1)}, u32[]{:S(2)}, u32[]{:S(2)}) %all-to-all-start.1) | async-done | bytes 207392 | tf_op jit(solution)/shard_map/all_to_all | solution.py:92
  113.7 3.9 %all-to-all-start.3 = ((f32[32,12,256]{2,1,0:T(8,128)}), f32[32,12,256]{2,1,0:T(8,128)S(1)}, u32[]{:S(2)}, u32[]{:S(2)}) async-start(f32[32,12,256]{2,1,0:T(8,128)} %reshape.148), calls=%async_computation.3 | async-start | bytes 1048576 | tf_op jit(solution)/shard_map/all_to_all | solution.py:145
  118.9 2.8 collective-permute-start
  121.9 21.9 %collective-permute-done.1 = f32[2,64,1]{2,1,0:T(8,128)S(1)} collective-permute-done((f32[2,64,1]{2,1,0:T(8,128)S(1)}, f32[2,64,1]{2,1,0:T(8,128)S(1)}, u32[]{:S(2)}, u32[]{:S(2)}) %collective-permute-start.1) | collective-permute-done | bytes 544 | tf_op jit(solution)/shard_map/ppermute | solution.py:23
  143.9 3.5 %collective-permute-start.3 = (f32[2,1,272]{2,1,0:T(1,128)S(1)}, f32[2,1,272]{2,1,0:T(1,128)S(1)}, u32[]{:S(2)}, u32[]{:S(2)}) collective-permute-start(f32[2,1,272]{2,1,0:T(1,128)S(1)} %get-tuple-element.22), channel_id=1, source_target_pairs={{0,32},{32,64},{64,96},{96,128},{128,160},{160,192},{192,224},{224... | collective-permute-start | bytes 6536 | tf_op jit(solution)/shard_map/ppermute | solution.py:23
  147.4 4.6 %collective-permute-start.2 = (f32[2,1,272]{2,1,0:T(1,128)S(1)}, f32[2,1,272]{2,1,0:T(1,128)S(1)}, u32[]{:S(2)}, u32[]{:S(2)}) collective-permute-start(f32[2,1,272]{2,1,0:T(1,128)S(1)} %get-tuple-element.21), channel_id=1, source_target_pairs={{32,0},{64,32},{96,64},{128,96},{160,128},{192,160},{224,192},{256... | collective-permute-start | bytes 6536 | tf_op jit(solution)/shard_map/ppermute | solution.py:25
  152.1 2.9 %scatter_custom_fusion.2 = f32[64,256]{1,0:T(8,128)S(1)} fusion(s32[384]{0:T(512)S(1)} %get-tuple-element.8, f32[384,256]{1,0:T(8,128)S(1)} %reshape.149, f32[]{:T(128)} %constant.76.clone.1, s32[384]{0:T(512)S(1)} %get-tuple-element.7), kind=kCustom, calls=%fused_computation.33 | custom fusion | flops 294912 | bytes 461824 | tf_op jit(solution)/shard_map/scatter-add | solution.py:159
  157.0 3.0 %collective-permute-done.4 = f32[1,64,1]{2,1,0:T(8,128)S(1)} collective-permute-done((f32[1,64,1]{2,1,0:T(8,128)S(1)}, f32[1,64,1]{2,1,0:T(8,128)S(1)}, u32[]{:S(2)}, u32[]{:S(2)}) %collective-permute-start.4) | collective-permute-done | bytes 288 | tf_op jit(solution)/shard_map/ppermute | solution.py:23
  160.0 4.5 %collective-permute-start.7 = (f32[1,1,272]{2,1,0:T(1,128)S(1)}, f32[1,1,272]{2,1,0:T(1,128)S(1)}, u32[]{:S(2)}, u32[]{:S(2)}) collective-permute-start(f32[1,1,272]{2,1,0:T(1,128)S(1)} %get-tuple-element.31), channel_id=1, source_target_pairs={{32,0},{64,32},{96,64},{128,96},{160,128},{192,160},{224,192},{256... | collective-permute-start | bytes 3272 | tf_op jit(solution)/shard_map/ppermute | solution.py:25
  164.5 1.9 collective-permute-start.6
  166.5 5.6 %collective-permute-done.6 = f32[1,1,272]{2,1,0:T(1,128)S(1)} collective-permute-done((f32[1,1,272]{2,1,0:T(1,128)S(1)}, f32[1,1,272]{2,1,0:T(1,128)S(1)}, u32[]{:S(2)}, u32[]{:S(2)}) %collective-permute-start.6) | collective-permute-done | bytes 1120 | tf_op jit(solution)/shard_map/ppermute | solution.py:23
  172.6 39.5 %all_to_all.50 = f32[3,64,270]{2,0,1:T(4,128)S(1)} all-to-all(f32[3,64,270]{2,0,1:T(4,128)S(1)} %copy.138), channel_id=1, replica_groups=mesh['band'=16,'lon'=32] {'lon'}, dimensions={1} | all-to-all | bytes 414720 | tf_op jit(solution)/shard_map/all_to_all | solution.py:89
  220.3 27.2 %all_to_all.51 = f32[32,3,2,270]{3,2,1,0:T(2,128)S(1)} all-to-all(f32[32,3,2,270]{3,2,1,0:T(2,128)S(1)} %constant_dynamic-update-slice_fusion.32), channel_id=1, replica_groups=mesh['band'=16,'lon'=32] {'lon'}, dimensions={0} | all-to-all | bytes 414720 | tf_op jit(solution)/shard_map/all_to_all | solution.py:92
  248.0 3.0 %collective-permute-start.8 = (f32[2,64,1]{2,1,0:T(8,128)S(1)}, f32[2,64,1]{2,1,0:T(8,128)S(1)}, u32[]{:S(2)}, u32[]{:S(2)}) collective-permute-start(f32[2,64,1]{2,1,0:T(8,128)S(1)} %get-tuple-element.24), channel_id=1, source_target_pairs={{1,0},{2,1},{3,2},{4,3},{5,4},{6,5},{7,6},{8,7},{9,8},{10,9},{11,1... | collective-permute-start | bytes 1544 | tf_op jit(solution)/shard_map/ppermute | solution.py:25
  251.0 1.9 collective-permute-done.9
  254.9 6.0 %collective-permute-start.10 = (f32[2,1,272]{2,1,0:T(1,128)S(1)}, f32[2,1,272]{2,1,0:T(1,128)S(1)}, u32[]{:S(2)}, u32[]{:S(2)}) collective-permute-start(f32[2,1,272]{2,1,0:T(1,128)S(1)} %get-tuple-element.19), channel_id=1, source_target_pairs={{32,0},{64,32},{96,64},{128,96},{160,128},{192,160},{224,192},{256... | collective-permute-start | bytes 6536 | tf_op jit(solution)/shard_map/ppermute | solution.py:25
  265.9 3.0 %collective-permute-done.12 = f32[1,64,1]{2,1,0:T(8,128)S(1)} collective-permute-done((f32[1,64,1]{2,1,0:T(8,128)S(1)}, f32[1,64,1]{2,1,0:T(8,128)S(1)}, u32[]{:S(2)}, u32[]{:S(2)}) %collective-permute-start.12) | collective-permute-done | bytes 288 | tf_op jit(solution)/shard_map/ppermute | solution.py:23
  269.0 6.0 %collective-permute-start.15 = (f32[1,1,272]{2,1,0:T(1,128)S(1)}, f32[1,1,272]{2,1,0:T(1,128)S(1)}, u32[]{:S(2)}, u32[]{:S(2)}) collective-permute-start(f32[1,1,272]{2,1,0:T(1,128)S(1)} %get-tuple-element.29), channel_id=1, source_target_pairs={{32,0},{64,32},{96,64},{128,96},{160,128},{192,160},{224,192},{256... | collective-permute-start | bytes 3272 | tf_op jit(solution)/shard_map/ppermute | solution.py:25
  275.0 1.9 collective-permute-start.14
  276.9 5.6 %collective-permute-done.14 = f32[1,1,272]{2,1,0:T(1,128)S(1)} collective-permute-done((f32[1,1,272]{2,1,0:T(1,128)S(1)}, f32[1,1,272]{2,1,0:T(1,128)S(1)}, u32[]{:S(2)}, u32[]{:S(2)}) %collective-permute-start.14) | collective-permute-done | bytes 1120 | tf_op jit(solution)/shard_map/ppermute | solution.py:23
  (171 shorter events, 56.2 us)
Async XLA Ops:
  0.6 1.1 copy-start.1
  2.7 43.7 %all-to-all-start = ((f32[3,64,270]{2,0,1:T(4,128)}), f32[3,64,270]{2,0,1:T(4,128)S(1)}, u32[]{:S(2)}, u32[]{:S(2)}) async-start(f32[3,64,270]{2,0,1:T(4,128)} %copy.129), calls=%async_computation | async-start | bytes 786432 | tf_op jit(solution)/shard_map/all_to_all | solution.py:89
  18.2 0.7 copy-start.4
  46.4 31.0 %all-to-all-start.2 = ((s32[32,12,2]{1,2,0:T(2,128)}), s32[32,12,2]{1,2,0:T(2,128)S(1)}, u32[]{:S(2)}, u32[]{:S(2)}) async-start(s32[32,12,2]{1,2,0:T(2,128)} %copy.136), calls=%async_computation.2 | async-start | bytes 65536 | tf_op jit(solution)/shard_map/all_to_all | solution.py:152
  77.4 36.3 %all-to-all-start.1 = ((f32[32,3,2,270]{3,2,1,0:T(2,128)}), f32[32,3,2,270]{3,2,1,0:T(2,128)S(1)}, u32[]{:S(2)}, u32[]{:S(2)}) async-start(f32[32,3,2,270]{3,2,1,0:T(2,128)} %constant_dynamic-update-slice_fusion), calls=%async_computation.1 | async-start | bytes 589824 | tf_op jit(solution)/shard_map/all_to_all | solution.py:92
  113.7 38.3 %all-to-all-start.3 = ((f32[32,12,256]{2,1,0:T(8,128)}), f32[32,12,256]{2,1,0:T(8,128)S(1)}, u32[]{:S(2)}, u32[]{:S(2)}) async-start(f32[32,12,256]{2,1,0:T(8,128)} %reshape.148), calls=%async_computation.3 | async-start | bytes 1048576 | tf_op jit(solution)/shard_map/all_to_all | solution.py:145
  117.6 0.7 copy-start.6
  118.8 25.0 %collective-permute-start.1 = (f32[2,64,1]{2,1,0:T(8,128)S(1)}, f32[2,64,1]{2,1,0:T(8,128)S(1)}, u32[]{:S(2)}, u32[]{:S(2)}) collective-permute-start(f32[2,64,1]{2,1,0:T(8,128)S(1)} %get-tuple-element.27), channel_id=1, source_target_pairs={{0,1},{1,2},{2,3},{3,4},{4,5},{5,6},{6,7},{7,8},{8,9},{9,10},{10,1... | collective-permute-start | bytes 1544 | tf_op jit(solution)/shard_map/ppermute | solution.py:23
  118.9 24.8 %collective-permute-start = (f32[2,64,1]{2,1,0:T(8,128)S(1)}, f32[2,64,1]{2,1,0:T(8,128)S(1)}, u32[]{:S(2)}, u32[]{:S(2)}) collective-permute-start(f32[2,64,1]{2,1,0:T(8,128)S(1)} %get-tuple-element.26), channel_id=1, source_target_pairs={{1,0},{2,1},{3,2},{4,3},{5,4},{6,5},{7,6},{8,7},{9,8},{10,9},{11,1... | collective-permute-start | bytes 1544 | tf_op jit(solution)/shard_map/ppermute | solution.py:25
  143.9 11.1 %collective-permute-start.3 = (f32[2,1,272]{2,1,0:T(1,128)S(1)}, f32[2,1,272]{2,1,0:T(1,128)S(1)}, u32[]{:S(2)}, u32[]{:S(2)}) collective-permute-start(f32[2,1,272]{2,1,0:T(1,128)S(1)} %get-tuple-element.22), channel_id=1, source_target_pairs={{0,32},{32,64},{64,96},{96,128},{128,160},{160,192},{192,224},{224... | collective-permute-start | bytes 6536 | tf_op jit(solution)/shard_map/ppermute | solution.py:23
  147.4 7.6 %collective-permute-start.2 = (f32[2,1,272]{2,1,0:T(1,128)S(1)}, f32[2,1,272]{2,1,0:T(1,128)S(1)}, u32[]{:S(2)}, u32[]{:S(2)}) collective-permute-start(f32[2,1,272]{2,1,0:T(1,128)S(1)} %get-tuple-element.21), channel_id=1, source_target_pairs={{32,0},{64,32},{96,64},{128,96},{160,128},{192,160},{224,192},{256... | collective-permute-start | bytes 6536 | tf_op jit(solution)/shard_map/ppermute | solution.py:25
  155.4 1.6 collective-permute-start.5
  155.4 4.6 %collective-permute-start.4 = (f32[1,64,1]{2,1,0:T(8,128)S(1)}, f32[1,64,1]{2,1,0:T(8,128)S(1)}, u32[]{:S(2)}, u32[]{:S(2)}) collective-permute-start(f32[1,64,1]{2,1,0:T(8,128)S(1)} %get-tuple-element.34), channel_id=1, source_target_pairs={{0,1},{1,2},{2,3},{3,4},{4,5},{5,6},{6,7},{7,8},{8,9},{9,10},{10,1... | collective-permute-start | bytes 776 | tf_op jit(solution)/shard_map/ppermute | solution.py:23
  160.0 6.5 %collective-permute-start.7 = (f32[1,1,272]{2,1,0:T(1,128)S(1)}, f32[1,1,272]{2,1,0:T(1,128)S(1)}, u32[]{:S(2)}, u32[]{:S(2)}) collective-permute-start(f32[1,1,272]{2,1,0:T(1,128)S(1)} %get-tuple-element.31), channel_id=1, source_target_pairs={{32,0},{64,32},{96,64},{128,96},{160,128},{192,160},{224,192},{256... | collective-permute-start | bytes 3272 | tf_op jit(solution)/shard_map/ppermute | solution.py:25
  164.5 7.6 %collective-permute-start.6 = (f32[1,1,272]{2,1,0:T(1,128)S(1)}, f32[1,1,272]{2,1,0:T(1,128)S(1)}, u32[]{:S(2)}, u32[]{:S(2)}) collective-permute-start(f32[1,1,272]{2,1,0:T(1,128)S(1)} %get-tuple-element.30), channel_id=1, source_target_pairs={{0,32},{32,64},{64,96},{96,128},{128,160},{160,192},{192,224},{224... | collective-permute-start | bytes 3272 | tf_op jit(solution)/shard_map/ppermute | solution.py:23
  166.5 5.7 %copy-start = (s32[64,270]{1,0:T(8,128)S(1)}, s32[64,270]{1,0:T(8,128)}, u32[]{:S(2)}) copy-start(s32[64,270]{1,0:T(8,128)} %param.19) | copy-start | bytes 207364
  248.0 4.9 %collective-permute-start.9 = (f32[2,64,1]{2,1,0:T(8,128)S(1)}, f32[2,64,1]{2,1,0:T(8,128)S(1)}, u32[]{:S(2)}, u32[]{:S(2)}) collective-permute-start(f32[2,64,1]{2,1,0:T(8,128)S(1)} %get-tuple-element.25), channel_id=1, source_target_pairs={{0,1},{1,2},{2,3},{3,4},{4,5},{5,6},{6,7},{7,8},{8,9},{9,10},{10,1... | collective-permute-start | bytes 1544 | tf_op jit(solution)/shard_map/ppermute | solution.py:23
  248.0 4.9 %collective-permute-start.8 = (f32[2,64,1]{2,1,0:T(8,128)S(1)}, f32[2,64,1]{2,1,0:T(8,128)S(1)}, u32[]{:S(2)}, u32[]{:S(2)}) collective-permute-start(f32[2,64,1]{2,1,0:T(8,128)S(1)} %get-tuple-element.24), channel_id=1, source_target_pairs={{1,0},{2,1},{3,2},{4,3},{5,4},{6,5},{7,6},{8,7},{9,8},{10,9},{11,1... | collective-permute-start | bytes 1544 | tf_op jit(solution)/shard_map/ppermute | solution.py:25
  253.0 8.0 %collective-permute-start.11 = (f32[2,1,272]{2,1,0:T(1,128)S(1)}, f32[2,1,272]{2,1,0:T(1,128)S(1)}, u32[]{:S(2)}, u32[]{:S(2)}) collective-permute-start(f32[2,1,272]{2,1,0:T(1,128)S(1)} %get-tuple-element.20), channel_id=1, source_target_pairs={{0,32},{32,64},{64,96},{96,128},{128,160},{160,192},{192,224},{224... | collective-permute-start | bytes 6536 | tf_op jit(solution)/shard_map/ppermute | solution.py:23
  254.9 7.3 %collective-permute-start.10 = (f32[2,1,272]{2,1,0:T(1,128)S(1)}, f32[2,1,272]{2,1,0:T(1,128)S(1)}, u32[]{:S(2)}, u32[]{:S(2)}) collective-permute-start(f32[2,1,272]{2,1,0:T(1,128)S(1)} %get-tuple-element.19), channel_id=1, source_target_pairs={{32,0},{64,32},{96,64},{128,96},{160,128},{192,160},{224,192},{256... | collective-permute-start | bytes 6536 | tf_op jit(solution)/shard_map/ppermute | solution.py:25
  262.5 3.4 %collective-permute-start.13 = (f32[1,64,1]{2,1,0:T(8,128)S(1)}, f32[1,64,1]{2,1,0:T(8,128)S(1)}, u32[]{:S(2)}, u32[]{:S(2)}) collective-permute-start(f32[1,64,1]{2,1,0:T(8,128)S(1)} %get-tuple-element.33), channel_id=1, source_target_pairs={{1,0},{2,1},{3,2},{4,3},{5,4},{6,5},{7,6},{8,7},{9,8},{10,9},{11,1... | collective-permute-start | bytes 776 | tf_op jit(solution)/shard_map/ppermute | solution.py:25
  264.3 4.6 %collective-permute-start.12 = (f32[1,64,1]{2,1,0:T(8,128)S(1)}, f32[1,64,1]{2,1,0:T(8,128)S(1)}, u32[]{:S(2)}, u32[]{:S(2)}) collective-permute-start(f32[1,64,1]{2,1,0:T(8,128)S(1)} %get-tuple-element.32), channel_id=1, source_target_pairs={{0,1},{1,2},{2,3},{3,4},{4,5},{5,6},{6,7},{7,8},{8,9},{9,10},{10,1... | collective-permute-start | bytes 776 | tf_op jit(solution)/shard_map/ppermute | solution.py:23
  269.0 7.9 %collective-permute-start.15 = (f32[1,1,272]{2,1,0:T(1,128)S(1)}, f32[1,1,272]{2,1,0:T(1,128)S(1)}, u32[]{:S(2)}, u32[]{:S(2)}) collective-permute-start(f32[1,1,272]{2,1,0:T(1,128)S(1)} %get-tuple-element.29), channel_id=1, source_target_pairs={{32,0},{64,32},{96,64},{128,96},{160,128},{192,160},{224,192},{256... | collective-permute-start | bytes 3272 | tf_op jit(solution)/shard_map/ppermute | solution.py:25
  275.0 7.6 %collective-permute-start.14 = (f32[1,1,272]{2,1,0:T(1,128)S(1)}, f32[1,1,272]{2,1,0:T(1,128)S(1)}, u32[]{:S(2)}, u32[]{:S(2)}) collective-permute-start(f32[1,1,272]{2,1,0:T(1,128)S(1)} %get-tuple-element.28), channel_id=1, source_target_pairs={{0,32},{32,64},{64,96},{96,128},{128,160},{160,192},{192,224},{224... | collective-permute-start | bytes 3272 | tf_op jit(solution)/shard_map/ppermute | solution.py:23
  (3 other events, 2.0 us)
